TPU v7x, 32 devices: a whole 2x2x4 slice. The times are simulated.
32 devices in a mesh: cases: 2 (over x), box: 16 (over z, y, core).
Axes of the slice: x: 2, y: 2, z: 4, core: 2. Of those that a mesh axis runs over, the one named last changes fastest.
Arguments:
- positions: float32 [2048, 3, 128], P(('cases', 'box')), parts along dimension 0, may hold values from -9 to 9, as said below
- strengths: float32 [2048, 3, 128], P(('cases', 'box')), parts along dimension 0, may hold values from -12 to 12
- history: float32 [2048, 2, 3, 128], P(('cases', 'box')), parts along dimension 0, may hold values from -5 to 5
- move_list: int32 [2048], P(('cases', 'box')), parts along dimension 0, may hold values from 0 to 1023, as said below
- age_slot: int32 [2048], P(('cases', 'box')), parts along dimension 0, may hold values from 0 to 1023, as said below
- fetch_list: int32 [32, 16, 8], P(('cases', 'box')), parts along dimension 0, may hold values from -1 to 63, as said below
- tile_slot: int32 [2048, 32], P(('cases', 'box')), parts along dimension 0, may hold values from 0 to 127, as said below
- tile_count: int32 [2048], P(('cases', 'box')), parts along dimension 0, may hold values from 1 to 32, as said below
- blade_id: int32 [2048, 128], P(('cases', 'box')), parts along dimension 0, may hold values from 0 to 17
- hub_centre: float32 [12, 3], P('cases'), parts along dimension 0, may hold values from -8 to 8
- azimuth: float32 [12], P('cases'), parts along dimension 0, may hold values from -3.140625 to 3.140625
Outputs:
- new_positions: float32 [2048, 3, 128], P(('cases', 'box')), parts along dimension 0
- new_history: float32 [2048, 2, 3, 128], P(('cases', 'box')), parts along dimension 0
- frame: float32 [2048, 3, 128], P(('cases', 'box')), parts along dimension 0
There are 2 independent parts, one for each index of `cases`. A program takes and returns all parts, laid end to end along the dimension named above; each array names one. Nothing has to cross between parts.
Inputs may be any that keep to these rules, and one draw needn't show every extreme that they name: Node positions; the first component of a block's nodes is offset by an amount that grows with the block's device. `move_list`: A permutation of block ids (block id = device * 64 + local block). Each device receives 64 blocks; the blocks of one device go at most 8 to any one device, and every device sends exactly 8 to some device. `age_slot`: A permutation of block ids, with the same bounds per pair of devices as move_list. `fetch_list`: entry [r, o, i] is -1 or a local block of device o; live entries come first in each [r, o] row and are distinct; rows [r, o] with o within two of r around the axis have 8 live entries. `tile_slot`: every entry names a live entry of fetch_list for the target block's device; tiles may repeat. `tile_count`: the first block of each device has 32.
All inputs are finite; a program needn't handle non-finite values.
Results may differ from a plain program's by a relative error of at most 0.0003.
Values sent between devices are 32-bit elements; how exact they have to be, the bound alone decides.
No kernel may reach another device: no remote copies, remote signals or barrier semaphores. Data moves between devices by JAX's collectives and lax.ppermute only.
A program may use at most 128 MiB of HBM per device.

v0:
```python
import math
import jax
import jax.numpy as jnp
from jax import lax
from jax.sharding import PartitionSpec as P

ROTORS = 6
BLADES = 3
core_square = 0.05
time_step = 0.05


def cross_product(first, second):
    return jnp.stack(
        [
            first[..., 1, :] * second[..., 2, :] - first[..., 2, :] * second[..., 1, :],
            first[..., 2, :] * second[..., 0, :] - first[..., 0, :] * second[..., 2, :],
            first[..., 0, :] * second[..., 1, :] - first[..., 1, :] * second[..., 0, :],
        ],
        axis=-2,
    )


def induced(target, source_pos, source_table, tile_mask):
    dist_sq = jnp.zeros((source_pos.shape[0], target.shape[-1], source_pos.shape[-1]), jnp.float32)
    for component in range(3):
        gap = target[component][None, :, None] - source_pos[:, component][:, None, :]
        dist_sq = dist_sq + gap * gap
    weight = tile_mask[:, None, None] * (dist_sq + core_square) ** (-1.5)
    summed = jnp.einsum("kij,kcj->ci", weight, source_table, precision=lax.Precision.HIGHEST)
    return (cross_product(target, summed[:3]) - summed[3:]) / (4.0 * math.pi)


def pack_blocks(values, targets, blocks, box_count, capacity):
    dest_box = targets // blocks
    dest_local = targets % blocks
    one_hot = (dest_box[:, None] == jnp.arange(box_count, dtype=jnp.int32)[None, :]).astype(
        jnp.int32
    )
    earlier = jnp.cumsum(one_hot, axis=0) - one_hot
    ranking = jnp.sum(earlier * one_hot, axis=1)
    place = dest_box * capacity + ranking
    buffer = (
        jnp.zeros((box_count * capacity,) + values.shape[1:], values.dtype).at[place].set(values)
    )
    labels = (
        jnp.full((box_count * capacity,), -1.0, jnp.float32)
        .at[place]
        .set(dest_local.astype(jnp.float32))
    )
    return (buffer, labels)


def unpack_blocks(arrived, labels, blocks):
    place = jnp.where(labels >= 0.0, labels, float(blocks)).astype(jnp.int32)
    return (
        jnp.zeros((blocks,) + arrived.shape[1:], arrived.dtype).at[place].set(arrived, mode="drop")
    )


def body(
    positions,
    strengths,
    history,
    move_list,
    age_slot,
    fetch_list,
    tile_slot,
    tile_count,
    blade_id,
    hub_centre,
    azimuth,
):
    blocks = positions.shape[0]
    box_count = lax.axis_size("box")
    capacity = 2 * blocks // box_count
    offered = jnp.concatenate([positions, strengths], axis=1)
    requests = fetch_list[0]
    everything = lax.all_gather(offered, "box", axis=0, tiled=True)
    wanted = jnp.arange(box_count, dtype=jnp.int32)[:, None] * blocks + jnp.clip(
        requests, 0, blocks - 1
    )
    fetched = jnp.take(everything, wanted.reshape(-1), axis=0)
    source_pos = fetched[:, :3]
    source_table = jnp.concatenate(
        [fetched[:, 3:], cross_product(fetched[:, :3], fetched[:, 3:])], axis=1
    )
    tile_mask = (
        jnp.arange(tile_slot.shape[1], dtype=jnp.int32)[None, :] < tile_count[:, None]
    ).astype(jnp.float32)

    def one_target(packed):
        target, slots, weights = packed
        return induced(
            target,
            jnp.take(source_pos, slots, axis=0),
            jnp.take(source_table, slots, axis=0),
            weights,
        )

    velocity = lax.map(one_target, (positions, tile_slot, tile_mask), batch_size=4)
    buffer, labels = pack_blocks(history, move_list, blocks, box_count, capacity)
    arrived, arrived_labels = (
        lax.all_to_all(buffer, "box", split_axis=0, concat_axis=0, tiled=True),
        lax.all_to_all(labels, "box", split_axis=0, concat_axis=0, tiled=True),
    )
    moved = unpack_blocks(arrived, arrived_labels, blocks)
    new_positions = (
        positions + time_step * (23.0 * velocity - 16.0 * moved[:, 0] + 5.0 * moved[:, 1]) / 12.0
    )
    new_history = jnp.stack([velocity, moved[:, 0]], axis=1)
    age_buffer, age_labels = pack_blocks(new_positions, age_slot, blocks, box_count, capacity)
    aged_in, aged_labels = (
        lax.all_to_all(age_buffer, "box", split_axis=0, concat_axis=0, tiled=True),
        lax.all_to_all(age_labels, "box", split_axis=0, concat_axis=0, tiled=True),
    )
    aged = unpack_blocks(aged_in, aged_labels, blocks)
    classes = ROTORS * BLADES
    blade_angle = (
        azimuth[:, None] + 2.0 * math.pi * jnp.arange(BLADES, dtype=jnp.float32)[None, :] / BLADES
    ).reshape(-1)
    centre_table = jnp.repeat(hub_centre, BLADES, axis=0)
    selector = (blade_id[None, :, :] == jnp.arange(classes, dtype=jnp.int32)[:, None, None]).astype(
        jnp.float32
    )
    cosine = jnp.sum(selector * jnp.cos(blade_angle)[:, None, None], axis=0)
    sine = jnp.sum(selector * jnp.sin(blade_angle)[:, None, None], axis=0)
    first = aged[:, 0] - jnp.sum(selector * centre_table[:, 0][:, None, None], axis=0)
    second = aged[:, 1] - jnp.sum(selector * centre_table[:, 1][:, None, None], axis=0)
    third = aged[:, 2] - jnp.sum(selector * centre_table[:, 2][:, None, None], axis=0)
    frame = jnp.stack(
        [cosine * first + sine * second, cosine * second - sine * first, third], axis=1
    )
    return (new_positions, new_history, frame)


def solution(mesh):
    placed = (
        P(("cases", "box"), None, None),
        P(("cases", "box"), None, None),
        P(("cases", "box"), None, None, None),
        P(("cases", "box")),
        P(("cases", "box")),
        P(("cases", "box"), None, None),
        P(("cases", "box"), None),
        P(("cases", "box")),
        P(("cases", "box"), None),
        P("cases", None),
        P("cases"),
    )
    return jax.shard_map(
        body,
        mesh=mesh,
        in_specs=placed,
        out_specs=(
            P(("cases", "box"), None, None),
            P(("cases", "box"), None, None, None),
            P(("cases", "box"), None, None),
        ),
        check_vma=False,
    )
```

profile of v0, /device:TPU:0, one launch (start us, length us, event | category | flops | bytes accessed | tf_op | source)
XLA Modules:
  0.0 342.8 jit_solution(4448846752251217391)
XLA Ops:
  7.2 1.6 pad_maximum_fusion.1
  9.9 0.8 scatter_custom_fusion
  11.4 7.4 %all-to-all-start = ((f32[16,8,1]{1,2,0:T(1,128)}), f32[16,8,1]{1,2,0:T(1,128)S(1)}, u32[]{:S(2)}, u32[]{:S(2)}) async-start(f32[16,8,1]{1,2,0:T(1,128)} %bitcast.25), calls=%async_computation | async-start | bytes 16384 | tf_op jit(solution)/shard_map/all_to_all | solution.py:105
  21.1 0.8 add_cosine_fusion
  22.6 0.8 copy.103
  23.4 0.8 scatter_custom_fusion.3
  24.8 0.8 broadcast_in_dim.91
  25.8 0.8 broadcast_in_dim.87
  26.7 8.0 %scatter_fusion = f32[128,2,3,128]{3,1,2,0:T(2,128)} fusion(f32[128,2,3,128]{3,1,2,0:T(2,128)} %broadcast_in_dim.87, s32[64]{0:T(128)S(1)} %compare_select_fusion.7, f32[64,2,3,128]{3,1,2,0:T(2,128)} %param.15), kind=kCustom, calls=%fused_computation.4 | custom fusion | bytes 590080 | tf_op jit(solution)/shard_map/scatter | solution.py:44
  34.7 6.0 %all-to-all-start.1 = ((f32[128,2,3,128]{3,1,2,0:T(2,128)}), f32[128,2,3,128]{3,1,2,0:T(2,128)S(1)}, u32[]{:S(2)}, u32[]{:S(2)}) async-start(f32[128,2,3,128]{3,1,2,0:T(2,128)} %scatter_fusion), calls=%async_computation.1 | async-start | bytes 786432 | tf_op jit(solution)/shard_map/all_to_all | solution.py:104
  42.1 17.4 %all-to-all-done.1 = f32[128,2,3,128]{3,1,2,0:T(2,128)S(1)} async-done(((f32[128,2,3,128]{3,1,2,0:T(2,128)}), f32[128,2,3,128]{3,1,2,0:T(2,128)S(1)}, u32[]{:S(2)}, u32[]{:S(2)}) %all-to-all-start.1) | async-done | bytes 393248 | tf_op jit(solution)/shard_map/all_to_all | solution.py:104
  59.5 6.2 %all-to-all-start.2 = ((f32[16,8,1]{1,2,0:T(1,128)}), f32[16,8,1]{1,2,0:T(1,128)S(1)}, u32[]{:S(2)}, u32[]{:S(2)}) async-start(f32[16,8,1]{1,2,0:T(1,128)} %bitcast.31), calls=%async_computation.2 | async-start | bytes 16384 | tf_op jit(solution)/shard_map/all_to_all | solution.py:115
  65.8 4.7 %scatter_fusion.1 = f32[64,2,3,128]{3,1,2,0:T(2,128)S(1)} fusion(f32[64,2,3,128]{3,1,2,0:T(2,128)S(1)} %broadcast_in_dim.84, s32[128]{0:T(128)S(1)} %fusion.44, f32[128,2,3,128]{3,1,2,0:T(2,128)S(1)} %all-to-all-done.1), kind=kCustom, calls=%fused_computation.5 | custom fusion | bytes 1180160 | tf_op jit(solution)/shard_map/scatter | solution.py:57
  70.7 5.7 %copy.106 = f32[1024,6,128]{2,1,0:T(8,128)} copy(f32[1024,6,128]{2,0,1:T(8,128)} %all-gather.2.cloned.1.call-done) | data formatting | bytes 6291456 | tf_op jit(solution)/shard_map/all_gather | solution.py:79
  76.4 2.9 gather_fusion.2
  80.2 226.8 %while.10 = (s32[]{:T(128)}, f32[16,4,3,128]{3,2,1,0:T(4,128)S(1)}, f32[16,4,3,128]{3,1,0,2:T(4,128)S(1)}, s32[16,4,32]{2,1,0:T(4,128)S(1)}, f32[128,6,128]{2,1,...) while((s32[]{:T(128)}, f32[16,4,3,128]{3,2,1,0:T(4,128)S(1)}, ...), condition=%wide.region_1.2_spmd, body=%wide.region_0.1_spmd.sunk | while | flops 172126848 | bytes 2662377 | solution.py:101
  80.5 0.8 gather_fusion
  81.6 0.8 gather_fusion.1
  82.4 12.0 %fusion.64 = f32[4,6,128]{2,1,0:T(8,128)S(1)} fusion(f32[4,32,128]{2,1,0:T(8,128)S(1)} %bitcast.126, f32[4,128]{1,0:T(4,128)S(1)} %get-tuple-element.200, f32[4,32,128]{2,1,0:T(8,128)S(1)} %bitcast.127, f32[4,128]{1,0:T(4,128)S(1)} %get-tuple-element.202, f32[4,32,128]{2,1,0:T(8,128)S(1)} %bitcast.125, f32[4,128]{1,0:T(4,128)S(1)} %get-tuple-element.204, ...), kind=kOutput, calls=%fused_computation.30.clone.1 | convolution fusion | flops 172064768 | bytes 608896 | tf_op jit(solution)/shard_map/while/body/eval_jaxpr/vmap(kij,kcj->ci)/dot_general | solution.py:30
  94.7 0.8 gather_fusion
  95.8 0.8 gather_fusion.1
  96.6 12.0 %fusion.64 = f32[4,6,128]{2,1,0:T(8,128)S(1)} fusion(f32[4,32,128]{2,1,0:T(8,128)S(1)} %bitcast.126, f32[4,128]{1,0:T(4,128)S(1)} %get-tuple-element.200, f32[4,32,128]{2,1,0:T(8,128)S(1)} %bitcast.127, f32[4,128]{1,0:T(4,128)S(1)} %get-tuple-element.202, f32[4,32,128]{2,1,0:T(8,128)S(1)} %bitcast.125, f32[4,128]{1,0:T(4,128)S(1)} %get-tuple-element.204, ...), kind=kOutput, calls=%fused_computation.30.clone.1 | convolution fusion | flops 172064768 | bytes 608896 | tf_op jit(solution)/shard_map/while/body/eval_jaxpr/vmap(kij,kcj->ci)/dot_general | solution.py:30
  108.8 0.8 gather_fusion
  110.0 0.8 gather_fusion.1
  110.8 12.0 %fusion.64 = f32[4,6,128]{2,1,0:T(8,128)S(1)} fusion(f32[4,32,128]{2,1,0:T(8,128)S(1)} %bitcast.126, f32[4,128]{1,0:T(4,128)S(1)} %get-tuple-element.200, f32[4,32,128]{2,1,0:T(8,128)S(1)} %bitcast.127, f32[4,128]{1,0:T(4,128)S(1)} %get-tuple-element.202, f32[4,32,128]{2,1,0:T(8,128)S(1)} %bitcast.125, f32[4,128]{1,0:T(4,128)S(1)} %get-tuple-element.204, ...), kind=kOutput, calls=%fused_computation.30.clone.1 | convolution fusion | flops 172064768 | bytes 608896 | tf_op jit(solution)/shard_map/while/body/eval_jaxpr/vmap(kij,kcj->ci)/dot_general | solution.py:30
  124.1 0.8 gather_fusion.1
  124.9 12.0 %fusion.64 = f32[4,6,128]{2,1,0:T(8,128)S(1)} fusion(f32[4,32,128]{2,1,0:T(8,128)S(1)} %bitcast.126, f32[4,128]{1,0:T(4,128)S(1)} %get-tuple-element.200, f32[4,32,128]{2,1,0:T(8,128)S(1)} %bitcast.127, f32[4,128]{1,0:T(4,128)S(1)} %get-tuple-element.202, f32[4,32,128]{2,1,0:T(8,128)S(1)} %bitcast.125, f32[4,128]{1,0:T(4,128)S(1)} %get-tuple-element.204, ...), kind=kOutput, calls=%fused_computation.30.clone.1 | convolution fusion | flops 172064768 | bytes 608896 | tf_op jit(solution)/shard_map/while/body/eval_jaxpr/vmap(kij,kcj->ci)/dot_general | solution.py:30
  138.3 0.8 gather_fusion.1
  139.1 12.0 %fusion.64 = f32[4,6,128]{2,1,0:T(8,128)S(1)} fusion(f32[4,32,128]{2,1,0:T(8,128)S(1)} %bitcast.126, f32[4,128]{1,0:T(4,128)S(1)} %get-tuple-element.200, f32[4,32,128]{2,1,0:T(8,128)S(1)} %bitcast.127, f32[4,128]{1,0:T(4,128)S(1)} %get-tuple-element.202, f32[4,32,128]{2,1,0:T(8,128)S(1)} %bitcast.125, f32[4,128]{1,0:T(4,128)S(1)} %get-tuple-element.204, ...), kind=kOutput, calls=%fused_computation.30.clone.1 | convolution fusion | flops 172064768 | bytes 608896 | tf_op jit(solution)/shard_map/while/body/eval_jaxpr/vmap(kij,kcj->ci)/dot_general | solution.py:30
  151.3 0.8 gather_fusion
  152.4 0.8 gather_fusion.1
  153.3 12.0 %fusion.64 = f32[4,6,128]{2,1,0:T(8,128)S(1)} fusion(f32[4,32,128]{2,1,0:T(8,128)S(1)} %bitcast.126, f32[4,128]{1,0:T(4,128)S(1)} %get-tuple-element.200, f32[4,32,128]{2,1,0:T(8,128)S(1)} %bitcast.127, f32[4,128]{1,0:T(4,128)S(1)} %get-tuple-element.202, f32[4,32,128]{2,1,0:T(8,128)S(1)} %bitcast.125, f32[4,128]{1,0:T(4,128)S(1)} %get-tuple-element.204, ...), kind=kOutput, calls=%fused_computation.30.clone.1 | convolution fusion | flops 172064768 | bytes 608896 | tf_op jit(solution)/shard_map/while/body/eval_jaxpr/vmap(kij,kcj->ci)/dot_general | solution.py:30
  166.6 0.8 gather_fusion.1
  167.4 12.0 %fusion.64 = f32[4,6,128]{2,1,0:T(8,128)S(1)} fusion(f32[4,32,128]{2,1,0:T(8,128)S(1)} %bitcast.126, f32[4,128]{1,0:T(4,128)S(1)} %get-tuple-element.200, f32[4,32,128]{2,1,0:T(8,128)S(1)} %bitcast.127, f32[4,128]{1,0:T(4,128)S(1)} %get-tuple-element.202, f32[4,32,128]{2,1,0:T(8,128)S(1)} %bitcast.125, f32[4,128]{1,0:T(4,128)S(1)} %get-tuple-element.204, ...), kind=kOutput, calls=%fused_computation.30.clone.1 | convolution fusion | flops 172064768 | bytes 608896 | tf_op jit(solution)/shard_map/while/body/eval_jaxpr/vmap(kij,kcj->ci)/dot_general | solution.py:30
  180.8 0.8 gather_fusion.1
  181.6 12.0 %fusion.64 = f32[4,6,128]{2,1,0:T(8,128)S(1)} fusion(f32[4,32,128]{2,1,0:T(8,128)S(1)} %bitcast.126, f32[4,128]{1,0:T(4,128)S(1)} %get-tuple-element.200, f32[4,32,128]{2,1,0:T(8,128)S(1)} %bitcast.127, f32[4,128]{1,0:T(4,128)S(1)} %get-tuple-element.202, f32[4,32,128]{2,1,0:T(8,128)S(1)} %bitcast.125, f32[4,128]{1,0:T(4,128)S(1)} %get-tuple-element.204, ...), kind=kOutput, calls=%fused_computation.30.clone.1 | convolution fusion | flops 172064768 | bytes 608896 | tf_op jit(solution)/shard_map/while/body/eval_jaxpr/vmap(kij,kcj->ci)/dot_general | solution.py:30
  193.8 0.8 gather_fusion
  194.9 0.8 gather_fusion.1
  195.8 12.0 %fusion.64 = f32[4,6,128]{2,1,0:T(8,128)S(1)} fusion(f32[4,32,128]{2,1,0:T(8,128)S(1)} %bitcast.126, f32[4,128]{1,0:T(4,128)S(1)} %get-tuple-element.200, f32[4,32,128]{2,1,0:T(8,128)S(1)} %bitcast.127, f32[4,128]{1,0:T(4,128)S(1)} %get-tuple-element.202, f32[4,32,128]{2,1,0:T(8,128)S(1)} %bitcast.125, f32[4,128]{1,0:T(4,128)S(1)} %get-tuple-element.204, ...), kind=kOutput, calls=%fused_computation.30.clone.1 | convolution fusion | flops 172064768 | bytes 608896 | tf_op jit(solution)/shard_map/while/body/eval_jaxpr/vmap(kij,kcj->ci)/dot_general | solution.py:30
  208.0 0.8 gather_fusion
  209.1 0.8 gather_fusion.1
  209.9 12.0 %fusion.64 = f32[4,6,128]{2,1,0:T(8,128)S(1)} fusion(f32[4,32,128]{2,1,0:T(8,128)S(1)} %bitcast.126, f32[4,128]{1,0:T(4,128)S(1)} %get-tuple-element.200, f32[4,32,128]{2,1,0:T(8,128)S(1)} %bitcast.127, f32[4,128]{1,0:T(4,128)S(1)} %get-tuple-element.202, f32[4,32,128]{2,1,0:T(8,128)S(1)} %bitcast.125, f32[4,128]{1,0:T(4,128)S(1)} %get-tuple-element.204, ...), kind=kOutput, calls=%fused_computation.30.clone.1 | convolution fusion | flops 172064768 | bytes 608896 | tf_op jit(solution)/shard_map/while/body/eval_jaxpr/vmap(kij,kcj->ci)/dot_general | solution.py:30
  222.1 0.8 gather_fusion
  223.3 0.8 gather_fusion.1
  224.1 12.0 %fusion.64 = f32[4,6,128]{2,1,0:T(8,128)S(1)} fusion(f32[4,32,128]{2,1,0:T(8,128)S(1)} %bitcast.126, f32[4,128]{1,0:T(4,128)S(1)} %get-tuple-element.200, f32[4,32,128]{2,1,0:T(8,128)S(1)} %bitcast.127, f32[4,128]{1,0:T(4,128)S(1)} %get-tuple-element.202, f32[4,32,128]{2,1,0:T(8,128)S(1)} %bitcast.125, f32[4,128]{1,0:T(4,128)S(1)} %get-tuple-element.204, ...), kind=kOutput, calls=%fused_computation.30.clone.1 | convolution fusion | flops 172064768 | bytes 608896 | tf_op jit(solution)/shard_map/while/body/eval_jaxpr/vmap(kij,kcj->ci)/dot_general | solution.py:30
  236.3 0.8 gather_fusion
  237.4 0.8 gather_fusion.1
  238.3 12.0 %fusion.64 = f32[4,6,128]{2,1,0:T(8,128)S(1)} fusion(f32[4,32,128]{2,1,0:T(8,128)S(1)} %bitcast.126, f32[4,128]{1,0:T(4,128)S(1)} %get-tuple-element.200, f32[4,32,128]{2,1,0:T(8,128)S(1)} %bitcast.127, f32[4,128]{1,0:T(4,128)S(1)} %get-tuple-element.202, f32[4,32,128]{2,1,0:T(8,128)S(1)} %bitcast.125, f32[4,128]{1,0:T(4,128)S(1)} %get-tuple-element.204, ...), kind=kOutput, calls=%fused_computation.30.clone.1 | convolution fusion | flops 172064768 | bytes 608896 | tf_op jit(solution)/shard_map/while/body/eval_jaxpr/vmap(kij,kcj->ci)/dot_general | solution.py:30
  251.6 0.8 gather_fusion.1
  252.4 12.0 %fusion.64 = f32[4,6,128]{2,1,0:T(8,128)S(1)} fusion(f32[4,32,128]{2,1,0:T(8,128)S(1)} %bitcast.126, f32[4,128]{1,0:T(4,128)S(1)} %get-tuple-element.200, f32[4,32,128]{2,1,0:T(8,128)S(1)} %bitcast.127, f32[4,128]{1,0:T(4,128)S(1)} %get-tuple-element.202, f32[4,32,128]{2,1,0:T(8,128)S(1)} %bitcast.125, f32[4,128]{1,0:T(4,128)S(1)} %get-tuple-element.204, ...), kind=kOutput, calls=%fused_computation.30.clone.1 | convolution fusion | flops 172064768 | bytes 608896 | tf_op jit(solution)/shard_map/while/body/eval_jaxpr/vmap(kij,kcj->ci)/dot_general | solution.py:30
  264.6 0.8 gather_fusion
  265.8 0.8 gather_fusion.1
  266.6 12.0 %fusion.64 = f32[4,6,128]{2,1,0:T(8,128)S(1)} fusion(f32[4,32,128]{2,1,0:T(8,128)S(1)} %bitcast.126, f32[4,128]{1,0:T(4,128)S(1)} %get-tuple-element.200, f32[4,32,128]{2,1,0:T(8,128)S(1)} %bitcast.127, f32[4,128]{1,0:T(4,128)S(1)} %get-tuple-element.202, f32[4,32,128]{2,1,0:T(8,128)S(1)} %bitcast.125, f32[4,128]{1,0:T(4,128)S(1)} %get-tuple-element.204, ...), kind=kOutput, calls=%fused_computation.30.clone.1 | convolution fusion | flops 172064768 | bytes 608896 | tf_op jit(solution)/shard_map/while/body/eval_jaxpr/vmap(kij,kcj->ci)/dot_general | solution.py:30
  278.8 0.8 gather_fusion
  279.9 0.8 gather_fusion.1
  280.7 12.0 %fusion.64 = f32[4,6,128]{2,1,0:T(8,128)S(1)} fusion(f32[4,32,128]{2,1,0:T(8,128)S(1)} %bitcast.126, f32[4,128]{1,0:T(4,128)S(1)} %get-tuple-element.200, f32[4,32,128]{2,1,0:T(8,128)S(1)} %bitcast.127, f32[4,128]{1,0:T(4,128)S(1)} %get-tuple-element.202, f32[4,32,128]{2,1,0:T(8,128)S(1)} %bitcast.125, f32[4,128]{1,0:T(4,128)S(1)} %get-tuple-element.204, ...), kind=kOutput, calls=%fused_computation.30.clone.1 | convolution fusion | flops 172064768 | bytes 608896 | tf_op jit(solution)/shard_map/while/body/eval_jaxpr/vmap(kij,kcj->ci)/dot_general | solution.py:30
  292.9 0.8 gather_fusion
  294.1 0.8 gather_fusion.1
  294.9 12.0 %fusion.64 = f32[4,6,128]{2,1,0:T(8,128)S(1)} fusion(f32[4,32,128]{2,1,0:T(8,128)S(1)} %bitcast.126, f32[4,128]{1,0:T(4,128)S(1)} %get-tuple-element.200, f32[4,32,128]{2,1,0:T(8,128)S(1)} %bitcast.127, f32[4,128]{1,0:T(4,128)S(1)} %get-tuple-element.202, f32[4,32,128]{2,1,0:T(8,128)S(1)} %bitcast.125, f32[4,128]{1,0:T(4,128)S(1)} %get-tuple-element.204, ...), kind=kOutput, calls=%fused_computation.30.clone.1 | convolution fusion | flops 172064768 | bytes 608896 | tf_op jit(solution)/shard_map/while/body/eval_jaxpr/vmap(kij,kcj->ci)/dot_general | solution.py:30
  307.9 6.6 %scatter_fusion.2 = f32[128,3,128]{2,1,0:T(4,128)} fusion(f32[128,3,128]{2,1,0:T(4,128)} %broadcast_in_dim.90, s32[64]{0:T(128)S(1)} %compare_select_fusion.4, f32[64,3,128]{2,1,0:T(4,128)S(1)} %copy.114), kind=kCustom, calls=%fused_computation.7 | custom fusion | bytes 295168 | tf_op jit(solution)/shard_map/scatter | solution.py:44
  314.5 6.0 %all-to-all-start.3 = ((f32[128,3,128]{2,1,0:T(4,128)}), f32[128,3,128]{2,1,0:T(4,128)S(1)}, u32[]{:S(2)}, u32[]{:S(2)}) async-start(f32[128,3,128]{2,1,0:T(4,128)} %scatter_fusion.2), calls=%async_computation.3 | async-start | bytes 524288 | tf_op jit(solution)/shard_map/all_to_all | solution.py:114
  321.6 0.8 copy.115
  322.5 8.1 %all-to-all-done.3 = f32[128,3,128]{2,1,0:T(4,128)S(1)} async-done(((f32[128,3,128]{2,1,0:T(4,128)}), f32[128,3,128]{2,1,0:T(4,128)S(1)}, u32[]{:S(2)}, u32[]{:S(2)}) %all-to-all-start.3) | async-done | bytes 196640 | tf_op jit(solution)/shard_map/all_to_all | solution.py:114
  330.6 4.5 %scatter_fusion.3 = f32[64,3,128]{2,1,0:T(4,128)S(1)} fusion(f32[64,3,128]{2,1,0:T(4,128)S(1)} %broadcast_in_dim.88, s32[128]{0:T(128)S(1)} %fusion.46, f32[128,3,128]{2,1,0:T(4,128)S(1)} %all-to-all-done.3), kind=kCustom, calls=%fused_computation.8 | custom fusion | bytes 590336 | tf_op jit(solution)/shard_map/scatter | solution.py:57
  (265 shorter events, 23.4 us)
Async XLA Ops:
  7.2 63.5 %all-gather.2.cloned.1.call-start = ((), (), s32[]{:S(2)}) async-start(), calls=%async_computation.4 | async-start | bytes 3342336 | tf_op jit(solution)/shard_map/all_gather | solution.py:79
  11.4 23.3 %all-to-all-start = ((f32[16,8,1]{1,2,0:T(1,128)}), f32[16,8,1]{1,2,0:T(1,128)S(1)}, u32[]{:S(2)}, u32[]{:S(2)}) async-start(f32[16,8,1]{1,2,0:T(1,128)} %bitcast.25), calls=%async_computation | async-start | bytes 16384 | tf_op jit(solution)/shard_map/all_to_all | solution.py:105
  34.7 24.8 %all-to-all-start.1 = ((f32[128,2,3,128]{3,1,2,0:T(2,128)}), f32[128,2,3,128]{3,1,2,0:T(2,128)S(1)}, u32[]{:S(2)}, u32[]{:S(2)}) async-start(f32[128,2,3,128]{3,1,2,0:T(2,128)} %scatter_fusion), calls=%async_computation.1 | async-start | bytes 786432 | tf_op jit(solution)/shard_map/all_to_all | solution.py:104
  59.5 255.0 %all-to-all-start.2 = ((f32[16,8,1]{1,2,0:T(1,128)}), f32[16,8,1]{1,2,0:T(1,128)S(1)}, u32[]{:S(2)}, u32[]{:S(2)}) async-start(f32[16,8,1]{1,2,0:T(1,128)} %bitcast.31), calls=%async_computation.2 | async-start | bytes 16384 | tf_op jit(solution)/shard_map/all_to_all | solution.py:115
  76.4 3.8 %copy-start = (f32[64,3,128]{2,0,1:T(8,128)S(1)}, f32[64,3,128]{2,0,1:T(8,128)}, u32[]{:S(2)}) copy-start(f32[64,3,128]{2,0,1:T(8,128)} %param.13) | copy-start | bytes 294916
  80.2 240.3 %copy-start.2 = (s32[64,128]{1,0:T(8,128)S(1)}, s32[64,128]{1,0:T(8,128)}, u32[]{:S(2)}) copy-start(s32[64,128]{1,0:T(8,128)} %param.21) | copy-start | bytes 98308
  307.1 28.9 %copy-start.1 = (f32[64,3,128]{2,0,1:T(8,128)}, f32[64,3,128]{2,0,1:T(8,128)S(1)}, u32[]{:S(2)}) copy-start(f32[64,3,128]{2,0,1:T(8,128)S(1)} %fusion.36) | copy-start | bytes 294916
  314.5 16.0 %all-to-all-start.3 = ((f32[128,3,128]{2,1,0:T(4,128)}), f32[128,3,128]{2,1,0:T(4,128)S(1)}, u32[]{:S(2)}, u32[]{:S(2)}) async-start(f32[128,3,128]{2,1,0:T(4,128)} %scatter_fusion.2), calls=%async_computation.3 | async-start | bytes 524288 | tf_op jit(solution)/shard_map/all_to_all | solution.py:114
Sparse Core Ops, SparseCore 0:
  10.8 54.3 all-gather.1
where the time goes:
time: 344 us; the launch traced here: 343 us
  matrix products  192 us (56%)
  local copies, waits for them, and re-layouts  70.9 us (21%)
  starting transfers between devices  25.7 us (7%)
  waiting for transfers between devices  25.5 us (7%)
  between operations  14.4 us (4%)
  other arithmetic  12.3 us (4%)
    dot_general x16, matrix products, induced(): jnp.einsum('kij,kcj->ci', weight, source_table, precision=lax.Precision.H...  192 us
    all_to_all x1, waiting for transfers between devices, body(): lax.all_to_all(buffer, 'box', split_axis=0, concat_axis=0, tiled=True)  17.4 us
    scatter x2, local copies, waits for them, and re-layouts, pack_blocks(): jnp.zeros((box_count * capacity,) + values.shape[1:], values.dtype)  14.5 us
    gather x16, local copies, waits for them, and re-layouts, one_target(): jnp.take(source_table, slots, axis=0)  12.2 us
    gather x16, local copies, waits for them, and re-layouts, one_target(): jnp.take(source_pos, slots, axis=0)  12 us
    scatter x2, local copies, waits for them, and re-layouts, unpack_blocks(): jnp.zeros((blocks,) + arrived.shape[1:], arrived.dtype).at[place]  9.19 us
    all_to_all x1, waiting for transfers between devices, body(): lax.all_to_all(age_buffer, 'box', split_axis=0, concat_axis=0, tiled=True)  8.07 us
    all_to_all x1, starting transfers between devices, body(): lax.all_to_all(labels, 'box', split_axis=0, concat_axis=0, tiled=True)  7.39 us
  transfers between devices with their start and end apart: 5, of which 2 were waited for; matrix products, arithmetic and copies ran while one was open for 78% of the time, Pallas kernels for 0%

commit v1 on v0

--- a/solution.py
+++ b/solution.py
@@ -8,6 +8,29 @@
 BLADES = 3
 core_square = 0.05
 time_step = 0.05
+
+
+def cut_along(x, dim, size):
+    lengths = x.shape
+    blocks = x.reshape(*lengths[:dim], size, lengths[dim] // size, *lengths[dim + 1 :])
+    return jnp.moveaxis(blocks, dim, 0)
+
+
+def laid_out(blocks, dim):
+    blocks = jnp.moveaxis(blocks, 0, dim)
+    dims = blocks.shape
+    return blocks.reshape(*dims[:dim], dims[dim] * dims[dim + 1], *dims[dim + 2 :])
+
+
+def exchange_directly(array, axis, split_dim, concat_dim):
+    size, index = (lax.axis_size(axis), lax.axis_index(axis))
+    blocks = cut_along(array, split_dim, size)
+    done = [blocks[index]]
+    for turn in range(1, size):
+        sent = blocks[(index + turn) % size]
+        done.append(lax.ppermute(sent, axis, [(i, (i + turn) % size) for i in range(size)]))
+    blocks = jnp.stack(done)[(index - jnp.arange(size)) % size]
+    return laid_out(blocks, concat_dim)
 
 
 def cross_product(first, second):
@@ -111,7 +134,7 @@
     new_history = jnp.stack([velocity, moved[:, 0]], axis=1)
     age_buffer, age_labels = pack_blocks(new_positions, age_slot, blocks, box_count, capacity)
     aged_in, aged_labels = (
-        lax.all_to_all(age_buffer, "box", split_axis=0, concat_axis=0, tiled=True),
+        exchange_directly(age_buffer, "box", 0, 0),
         lax.all_to_all(age_labels, "box", split_axis=0, concat_axis=0, tiled=True),
     )
     aged = unpack_blocks(aged_in, aged_labels, blocks)

time: 344 us -> 347 us (level)
  starting transfers between devices: 25.7 us -> 40.1 us
  waiting for transfers between devices: 25.5 us -> 16.6 us
  local copies, waits for them, and re-layouts: 70.9 us -> 67.1 us
    ppermute x0 -> x15, starting transfers between devices: none -> 20.9 us  [exchange_directly(): lax.ppermute(sent, axis, [(i, (i + turn) % size) for i in range(size)])]
    all_to_all x1 -> x0, waiting for transfers between devices: 8.07 us -> none  [body(): lax.all_to_all(age_buffer, 'box', split_axis=0, concat_axis=0, tiled=True)]
    all_to_all x1 -> x0, starting transfers between devices: 5.99 us -> none  [body(): lax.all_to_all(age_buffer, 'box', split_axis=0, concat_axis=0, tiled=True)]
    scatter x2 -> x3, local copies, waits for them, and re-layouts: 14.5 us -> 10.6 us  [pack_blocks(): jnp.zeros((box_count * capacity,) + values.shape[1:], values.dtype)]
  transfers between devices with their start and end apart: 5 -> 19, of which waited for: 2 -> 3; matrix products, arithmetic and copies ran while one was open for 78% -> 7% of each run, Pallas kernels for 0% -> 0%
where the time goes in v1:
time: 347 us; the launch traced here: 346 us
  matrix products  192 us (55%)
  local copies, waits for them, and re-layouts  67.1 us (19%)
  starting transfers between devices  40.1 us (12%)
  waiting for transfers between devices  16.6 us (5%)
  between operations  14.8 us (4%)
  other arithmetic  13.1 us (4%)
    dot_general x16, matrix products, induced(): jnp.einsum('kij,kcj->ci', weight, source_table, precision=lax.Precision.H...  192 us
    ppermute x15, starting transfers between devices, exchange_directly(): lax.ppermute(sent, axis, [(i, (i + turn) % size) for i in range(size)])  20.9 us
    all_to_all x1, waiting for transfers between devices, body(): lax.all_to_all(buffer, 'box', split_axis=0, concat_axis=0, tiled=True)  14.3 us
    gather x16, local copies, waits for them, and re-layouts, one_target(): jnp.take(source_table, slots, axis=0)  12.2 us
    gather x16, local copies, waits for them, and re-layouts, one_target(): jnp.take(source_pos, slots, axis=0)  12 us
    scatter x3, local copies, waits for them, and re-layouts, pack_blocks(): jnp.zeros((box_count * capacity,) + values.shape[1:], values.dtype)  10.6 us
    scatter x2, local copies, waits for them, and re-layouts, unpack_blocks(): jnp.zeros((blocks,) + arrived.shape[1:], arrived.dtype).at[place]  9.19 us
    all_to_all x1, starting transfers between devices, body(): lax.all_to_all(labels, 'box', split_axis=0, concat_axis=0, tiled=True)  7.39 us
  transfers between devices with their start and end apart: 19, of which 3 were waited for; matrix products, arithmetic and copies ran while one was open for 7% of the time, Pallas kernels for 0%

profile of v1, /device:TPU:0, one launch (start us, length us, event | category | flops | bytes accessed | tf_op | source)
XLA Modules:
  0.0 345.7 jit_solution(16363712468963476601)
XLA Ops:
  7.2 1.6 pad_maximum_fusion.1
  10.9 0.8 scatter_custom_fusion
  12.4 7.4 %all-to-all-start = ((f32[16,8,1]{1,2,0:T(1,128)}), f32[16,8,1]{1,2,0:T(1,128)S(1)}, u32[]{:S(2)}, u32[]{:S(2)}) async-start(f32[16,8,1]{1,2,0:T(1,128)} %bitcast.25), calls=%async_computation | async-start | bytes 16384 | tf_op jit(solution)/shard_map/all_to_all | solution.py:128
  21.2 0.8 broadcast_in_dim.92
  22.0 0.8 add_cosine_fusion
  23.0 1.0 select_reduce_fusion.1
  24.8 0.8 copy.135
  25.7 0.8 scatter_custom_fusion.3
  27.1 5.8 %all-to-all-start.2 = ((f32[16,8,1]{1,2,0:T(1,128)}), f32[16,8,1]{1,2,0:T(1,128)S(1)}, u32[]{:S(2)}, u32[]{:S(2)}) async-start(f32[16,8,1]{1,2,0:T(1,128)} %bitcast.31), calls=%async_computation.2 | async-start | bytes 16384 | tf_op jit(solution)/shard_map/all_to_all | solution.py:138
  33.0 0.8 broadcast_in_dim.88
  33.9 8.0 %scatter_fusion = f32[128,2,3,128]{3,1,2,0:T(2,128)} fusion(f32[128,2,3,128]{3,1,2,0:T(2,128)} %broadcast_in_dim.88, s32[64]{0:T(128)S(1)} %get-tuple-element.170, f32[64,2,3,128]{3,1,2,0:T(2,128)} %param.15), kind=kCustom, calls=%fused_computation.5 | custom fusion | bytes 590080 | tf_op jit(solution)/shard_map/scatter | solution.py:67
  41.9 6.0 %all-to-all-start.1 = ((f32[128,2,3,128]{3,1,2,0:T(2,128)}), f32[128,2,3,128]{3,1,2,0:T(2,128)S(1)}, u32[]{:S(2)}, u32[]{:S(2)}) async-start(f32[128,2,3,128]{3,1,2,0:T(2,128)} %scatter_fusion), calls=%async_computation.1 | async-start | bytes 786432 | tf_op jit(solution)/shard_map/all_to_all | solution.py:127
  50.0 14.3 %all-to-all-done.1 = f32[128,2,3,128]{3,1,2,0:T(2,128)S(1)} async-done(((f32[128,2,3,128]{3,1,2,0:T(2,128)}), f32[128,2,3,128]{3,1,2,0:T(2,128)S(1)}, u32[]{:S(2)}, u32[]{:S(2)}) %all-to-all-start.1) | async-done | bytes 393248 | tf_op jit(solution)/shard_map/all_to_all | solution.py:127
  64.3 4.7 %scatter_fusion.1 = f32[64,2,3,128]{3,1,2,0:T(2,128)S(1)} fusion(f32[64,2,3,128]{3,1,2,0:T(2,128)S(1)} %broadcast_in_dim.85, s32[128]{0:T(128)S(1)} %fusion.45, f32[128,2,3,128]{3,1,2,0:T(2,128)S(1)} %all-to-all-done.1), kind=kCustom, calls=%fused_computation.6 | custom fusion | bytes 1180160 | tf_op jit(solution)/shard_map/scatter | solution.py:80
  69.2 5.7 %copy.138 = f32[1024,6,128]{2,1,0:T(8,128)} copy(f32[1024,6,128]{2,0,1:T(8,128)} %all-gather.2.cloned.1.call-done) | data formatting | bytes 6291456 | tf_op jit(solution)/shard_map/all_gather | solution.py:102
  75.0 2.9 gather_fusion.2
  78.7 226.8 %while.10 = (s32[]{:T(128)}, f32[16,4,3,128]{3,2,1,0:T(4,128)S(1)}, f32[16,4,3,128]{3,1,0,2:T(4,128)S(1)}, s32[16,4,32]{2,1,0:T(4,128)S(1)}, f32[128,6,128]{2,1,...) while((s32[]{:T(128)}, f32[16,4,3,128]{3,2,1,0:T(4,128)S(1)}, ...), condition=%wide.region_1.2_spmd, body=%wide.region_0.1_spmd.sunk | while | flops 172126848 | bytes 2662377 | solution.py:124
  80.2 0.8 gather_fusion.1
  81.0 12.0 %fusion.66 = f32[4,6,128]{2,1,0:T(8,128)S(1)} fusion(f32[4,32,128]{2,1,0:T(8,128)S(1)} %bitcast.196, f32[4,128]{1,0:T(4,128)S(1)} %get-tuple-element.227, f32[4,32,128]{2,1,0:T(8,128)S(1)} %bitcast.197, f32[4,128]{1,0:T(4,128)S(1)} %get-tuple-element.229, f32[4,32,128]{2,1,0:T(8,128)S(1)} %bitcast.195, f32[4,128]{1,0:T(4,128)S(1)} %get-tuple-element.231, ...), kind=kOutput, calls=%fused_computation.31.clone.1 | convolution fusion | flops 172064768 | bytes 608896 | tf_op jit(solution)/shard_map/while/body/eval_jaxpr/vmap(kij,kcj->ci)/dot_general | solution.py:53
  94.3 0.8 gather_fusion.1
  95.2 12.0 %fusion.66 = f32[4,6,128]{2,1,0:T(8,128)S(1)} fusion(f32[4,32,128]{2,1,0:T(8,128)S(1)} %bitcast.196, f32[4,128]{1,0:T(4,128)S(1)} %get-tuple-element.227, f32[4,32,128]{2,1,0:T(8,128)S(1)} %bitcast.197, f32[4,128]{1,0:T(4,128)S(1)} %get-tuple-element.229, f32[4,32,128]{2,1,0:T(8,128)S(1)} %bitcast.195, f32[4,128]{1,0:T(4,128)S(1)} %get-tuple-element.231, ...), kind=kOutput, calls=%fused_computation.31.clone.1 | convolution fusion | flops 172064768 | bytes 608896 | tf_op jit(solution)/shard_map/while/body/eval_jaxpr/vmap(kij,kcj->ci)/dot_general | solution.py:53
  108.5 0.8 gather_fusion.1
  109.3 12.0 %fusion.66 = f32[4,6,128]{2,1,0:T(8,128)S(1)} fusion(f32[4,32,128]{2,1,0:T(8,128)S(1)} %bitcast.196, f32[4,128]{1,0:T(4,128)S(1)} %get-tuple-element.227, f32[4,32,128]{2,1,0:T(8,128)S(1)} %bitcast.197, f32[4,128]{1,0:T(4,128)S(1)} %get-tuple-element.229, f32[4,32,128]{2,1,0:T(8,128)S(1)} %bitcast.195, f32[4,128]{1,0:T(4,128)S(1)} %get-tuple-element.231, ...), kind=kOutput, calls=%fused_computation.31.clone.1 | convolution fusion | flops 172064768 | bytes 608896 | tf_op jit(solution)/shard_map/while/body/eval_jaxpr/vmap(kij,kcj->ci)/dot_general | solution.py:53
  122.7 0.8 gather_fusion.1
  123.5 12.0 %fusion.66 = f32[4,6,128]{2,1,0:T(8,128)S(1)} fusion(f32[4,32,128]{2,1,0:T(8,128)S(1)} %bitcast.196, f32[4,128]{1,0:T(4,128)S(1)} %get-tuple-element.227, f32[4,32,128]{2,1,0:T(8,128)S(1)} %bitcast.197, f32[4,128]{1,0:T(4,128)S(1)} %get-tuple-element.229, f32[4,32,128]{2,1,0:T(8,128)S(1)} %bitcast.195, f32[4,128]{1,0:T(4,128)S(1)} %get-tuple-element.231, ...), kind=kOutput, calls=%fused_computation.31.clone.1 | convolution fusion | flops 172064768 | bytes 608896 | tf_op jit(solution)/shard_map/while/body/eval_jaxpr/vmap(kij,kcj->ci)/dot_general | solution.py:53
  136.8 0.8 gather_fusion.1
  137.7 12.0 %fusion.66 = f32[4,6,128]{2,1,0:T(8,128)S(1)} fusion(f32[4,32,128]{2,1,0:T(8,128)S(1)} %bitcast.196, f32[4,128]{1,0:T(4,128)S(1)} %get-tuple-element.227, f32[4,32,128]{2,1,0:T(8,128)S(1)} %bitcast.197, f32[4,128]{1,0:T(4,128)S(1)} %get-tuple-element.229, f32[4,32,128]{2,1,0:T(8,128)S(1)} %bitcast.195, f32[4,128]{1,0:T(4,128)S(1)} %get-tuple-element.231, ...), kind=kOutput, calls=%fused_computation.31.clone.1 | convolution fusion | flops 172064768 | bytes 608896 | tf_op jit(solution)/shard_map/while/body/eval_jaxpr/vmap(kij,kcj->ci)/dot_general | solution.py:53
  151.0 0.8 gather_fusion.1
  151.8 12.0 %fusion.66 = f32[4,6,128]{2,1,0:T(8,128)S(1)} fusion(f32[4,32,128]{2,1,0:T(8,128)S(1)} %bitcast.196, f32[4,128]{1,0:T(4,128)S(1)} %get-tuple-element.227, f32[4,32,128]{2,1,0:T(8,128)S(1)} %bitcast.197, f32[4,128]{1,0:T(4,128)S(1)} %get-tuple-element.229, f32[4,32,128]{2,1,0:T(8,128)S(1)} %bitcast.195, f32[4,128]{1,0:T(4,128)S(1)} %get-tuple-element.231, ...), kind=kOutput, calls=%fused_computation.31.clone.1 | convolution fusion | flops 172064768 | bytes 608896 | tf_op jit(solution)/shard_map/while/body/eval_jaxpr/vmap(kij,kcj->ci)/dot_general | solution.py:53
  165.2 0.8 gather_fusion.1
  166.0 12.0 %fusion.66 = f32[4,6,128]{2,1,0:T(8,128)S(1)} fusion(f32[4,32,128]{2,1,0:T(8,128)S(1)} %bitcast.196, f32[4,128]{1,0:T(4,128)S(1)} %get-tuple-element.227, f32[4,32,128]{2,1,0:T(8,128)S(1)} %bitcast.197, f32[4,128]{1,0:T(4,128)S(1)} %get-tuple-element.229, f32[4,32,128]{2,1,0:T(8,128)S(1)} %bitcast.195, f32[4,128]{1,0:T(4,128)S(1)} %get-tuple-element.231, ...), kind=kOutput, calls=%fused_computation.31.clone.1 | convolution fusion | flops 172064768 | bytes 608896 | tf_op jit(solution)/shard_map/while/body/eval_jaxpr/vmap(kij,kcj->ci)/dot_general | solution.py:53
  179.3 0.8 gather_fusion.1
  180.1 12.0 %fusion.66 = f32[4,6,128]{2,1,0:T(8,128)S(1)} fusion(f32[4,32,128]{2,1,0:T(8,128)S(1)} %bitcast.196, f32[4,128]{1,0:T(4,128)S(1)} %get-tuple-element.227, f32[4,32,128]{2,1,0:T(8,128)S(1)} %bitcast.197, f32[4,128]{1,0:T(4,128)S(1)} %get-tuple-element.229, f32[4,32,128]{2,1,0:T(8,128)S(1)} %bitcast.195, f32[4,128]{1,0:T(4,128)S(1)} %get-tuple-element.231, ...), kind=kOutput, calls=%fused_computation.31.clone.1 | convolution fusion | flops 172064768 | bytes 608896 | tf_op jit(solution)/shard_map/while/body/eval_jaxpr/vmap(kij,kcj->ci)/dot_general | solution.py:53
  193.5 0.8 gather_fusion.1
  194.3 12.0 %fusion.66 = f32[4,6,128]{2,1,0:T(8,128)S(1)} fusion(f32[4,32,128]{2,1,0:T(8,128)S(1)} %bitcast.196, f32[4,128]{1,0:T(4,128)S(1)} %get-tuple-element.227, f32[4,32,128]{2,1,0:T(8,128)S(1)} %bitcast.197, f32[4,128]{1,0:T(4,128)S(1)} %get-tuple-element.229, f32[4,32,128]{2,1,0:T(8,128)S(1)} %bitcast.195, f32[4,128]{1,0:T(4,128)S(1)} %get-tuple-element.231, ...), kind=kOutput, calls=%fused_computation.31.clone.1 | convolution fusion | flops 172064768 | bytes 608896 | tf_op jit(solution)/shard_map/while/body/eval_jaxpr/vmap(kij,kcj->ci)/dot_general | solution.py:53
  207.7 0.8 gather_fusion.1
  208.5 12.0 %fusion.66 = f32[4,6,128]{2,1,0:T(8,128)S(1)} fusion(f32[4,32,128]{2,1,0:T(8,128)S(1)} %bitcast.196, f32[4,128]{1,0:T(4,128)S(1)} %get-tuple-element.227, f32[4,32,128]{2,1,0:T(8,128)S(1)} %bitcast.197, f32[4,128]{1,0:T(4,128)S(1)} %get-tuple-element.229, f32[4,32,128]{2,1,0:T(8,128)S(1)} %bitcast.195, f32[4,128]{1,0:T(4,128)S(1)} %get-tuple-element.231, ...), kind=kOutput, calls=%fused_computation.31.clone.1 | convolution fusion | flops 172064768 | bytes 608896 | tf_op jit(solution)/shard_map/while/body/eval_jaxpr/vmap(kij,kcj->ci)/dot_general | solution.py:53
  221.8 0.8 gather_fusion.1
  222.6 12.0 %fusion.66 = f32[4,6,128]{2,1,0:T(8,128)S(1)} fusion(f32[4,32,128]{2,1,0:T(8,128)S(1)} %bitcast.196, f32[4,128]{1,0:T(4,128)S(1)} %get-tuple-element.227, f32[4,32,128]{2,1,0:T(8,128)S(1)} %bitcast.197, f32[4,128]{1,0:T(4,128)S(1)} %get-tuple-element.229, f32[4,32,128]{2,1,0:T(8,128)S(1)} %bitcast.195, f32[4,128]{1,0:T(4,128)S(1)} %get-tuple-element.231, ...), kind=kOutput, calls=%fused_computation.31.clone.1 | convolution fusion | flops 172064768 | bytes 608896 | tf_op jit(solution)/shard_map/while/body/eval_jaxpr/vmap(kij,kcj->ci)/dot_general | solution.py:53
  236.0 0.8 gather_fusion.1
  236.8 12.0 %fusion.66 = f32[4,6,128]{2,1,0:T(8,128)S(1)} fusion(f32[4,32,128]{2,1,0:T(8,128)S(1)} %bitcast.196, f32[4,128]{1,0:T(4,128)S(1)} %get-tuple-element.227, f32[4,32,128]{2,1,0:T(8,128)S(1)} %bitcast.197, f32[4,128]{1,0:T(4,128)S(1)} %get-tuple-element.229, f32[4,32,128]{2,1,0:T(8,128)S(1)} %bitcast.195, f32[4,128]{1,0:T(4,128)S(1)} %get-tuple-element.231, ...), kind=kOutput, calls=%fused_computation.31.clone.1 | convolution fusion | flops 172064768 | bytes 608896 | tf_op jit(solution)/shard_map/while/body/eval_jaxpr/vmap(kij,kcj->ci)/dot_general | solution.py:53
  250.1 0.8 gather_fusion.1
  251.0 12.0 %fusion.66 = f32[4,6,128]{2,1,0:T(8,128)S(1)} fusion(f32[4,32,128]{2,1,0:T(8,128)S(1)} %bitcast.196, f32[4,128]{1,0:T(4,128)S(1)} %get-tuple-element.227, f32[4,32,128]{2,1,0:T(8,128)S(1)} %bitcast.197, f32[4,128]{1,0:T(4,128)S(1)} %get-tuple-element.229, f32[4,32,128]{2,1,0:T(8,128)S(1)} %bitcast.195, f32[4,128]{1,0:T(4,128)S(1)} %get-tuple-element.231, ...), kind=kOutput, calls=%fused_computation.31.clone.1 | convolution fusion | flops 172064768 | bytes 608896 | tf_op jit(solution)/shard_map/while/body/eval_jaxpr/vmap(kij,kcj->ci)/dot_general | solution.py:53
  264.3 0.8 gather_fusion.1
  265.1 12.0 %fusion.66 = f32[4,6,128]{2,1,0:T(8,128)S(1)} fusion(f32[4,32,128]{2,1,0:T(8,128)S(1)} %bitcast.196, f32[4,128]{1,0:T(4,128)S(1)} %get-tuple-element.227, f32[4,32,128]{2,1,0:T(8,128)S(1)} %bitcast.197, f32[4,128]{1,0:T(4,128)S(1)} %get-tuple-element.229, f32[4,32,128]{2,1,0:T(8,128)S(1)} %bitcast.195, f32[4,128]{1,0:T(4,128)S(1)} %get-tuple-element.231, ...), kind=kOutput, calls=%fused_computation.31.clone.1 | convolution fusion | flops 172064768 | bytes 608896 | tf_op jit(solution)/shard_map/while/body/eval_jaxpr/vmap(kij,kcj->ci)/dot_general | solution.py:53
  277.3 0.8 gather_fusion
  278.5 0.8 gather_fusion.1
  279.3 12.0 %fusion.66 = f32[4,6,128]{2,1,0:T(8,128)S(1)} fusion(f32[4,32,128]{2,1,0:T(8,128)S(1)} %bitcast.196, f32[4,128]{1,0:T(4,128)S(1)} %get-tuple-element.227, f32[4,32,128]{2,1,0:T(8,128)S(1)} %bitcast.197, f32[4,128]{1,0:T(4,128)S(1)} %get-tuple-element.229, f32[4,32,128]{2,1,0:T(8,128)S(1)} %bitcast.195, f32[4,128]{1,0:T(4,128)S(1)} %get-tuple-element.231, ...), kind=kOutput, calls=%fused_computation.31.clone.1 | convolution fusion | flops 172064768 | bytes 608896 | tf_op jit(solution)/shard_map/while/body/eval_jaxpr/vmap(kij,kcj->ci)/dot_general | solution.py:53
  292.6 0.8 gather_fusion.1
  293.5 12.0 %fusion.66 = f32[4,6,128]{2,1,0:T(8,128)S(1)} fusion(f32[4,32,128]{2,1,0:T(8,128)S(1)} %bitcast.196, f32[4,128]{1,0:T(4,128)S(1)} %get-tuple-element.227, f32[4,32,128]{2,1,0:T(8,128)S(1)} %bitcast.197, f32[4,128]{1,0:T(4,128)S(1)} %get-tuple-element.229, f32[4,32,128]{2,1,0:T(8,128)S(1)} %bitcast.195, f32[4,128]{1,0:T(4,128)S(1)} %get-tuple-element.231, ...), kind=kOutput, calls=%fused_computation.31.clone.1 | convolution fusion | flops 172064768 | bytes 608896 | tf_op jit(solution)/shard_map/while/body/eval_jaxpr/vmap(kij,kcj->ci)/dot_general | solution.py:53
  305.8 2.7 scatter_fusion.2
  308.8 1.5 collective-permute-start.1
  310.3 1.9 collective-permute-start.2
  312.7 0.8 copy.151
  313.6 0.9 collective-permute-done
  314.5 1.8 collective-permute-start.5
  316.3 2.2 collective-permute-start.6
  318.5 2.0 collective-permute-start.7
  320.6 1.8 collective-permute-start.9
  322.4 3.7 %collective-permute-start.10 = (f32[8,3,128]{2,0,1:T(8,128)S(1)}, f32[8,3,128]{2,0,1:T(8,128)S(1)}, u32[]{:S(2)}, u32[]{:S(2)}) collective-permute-start(f32[8,3,128]{2,0,1:T(8,128)S(1)} %get-tuple-element.146), channel_id=1, source_target_pairs={{0,11},{1,12},{2,13},{3,14},{4,15},{5,0},{6,1},{7,2},{8,3},{9,4},{... | collective-permute-start | bytes 36872 | tf_op jit(solution)/shard_map/ppermute | solution.py:31
  327.0 1.6 collective-permute-start.13
  328.6 2.6 collective-permute-start.14
  331.4 1.3 collective-permute-done.14
  333.5 4.5 %scatter_fusion.3 = f32[64,3,128]{2,1,0:T(4,128)S(1)} fusion(f32[64,3,128]{2,1,0:T(4,128)S(1)} %broadcast_in_dim.89, s32[128]{0:T(128)S(1)} %fusion.47, f32[128,3,128]{2,1,0:T(4,128)S(1)} %copy.150), kind=kCustom, calls=%fused_computation.9 | custom fusion | bytes 590336 | tf_op jit(solution)/shard_map/scatter | solution.py:80
  (313 shorter events, 32.5 us)
Async XLA Ops:
  7.2 62.1 %all-gather.2.cloned.1.call-start = ((), (), s32[]{:S(2)}) async-start(), calls=%async_computation.3 | async-start | bytes 3342336 | tf_op jit(solution)/shard_map/all_gather | solution.py:102
  12.4 14.7 %all-to-all-start = ((f32[16,8,1]{1,2,0:T(1,128)}), f32[16,8,1]{1,2,0:T(1,128)S(1)}, u32[]{:S(2)}, u32[]{:S(2)}) async-start(f32[16,8,1]{1,2,0:T(1,128)} %bitcast.25), calls=%async_computation | async-start | bytes 16384 | tf_op jit(solution)/shard_map/all_to_all | solution.py:128
  27.1 14.7 %all-to-all-start.2 = ((f32[16,8,1]{1,2,0:T(1,128)}), f32[16,8,1]{1,2,0:T(1,128)S(1)}, u32[]{:S(2)}, u32[]{:S(2)}) async-start(f32[16,8,1]{1,2,0:T(1,128)} %bitcast.31), calls=%async_computation.2 | async-start | bytes 16384 | tf_op jit(solution)/shard_map/all_to_all | solution.py:138
  41.9 22.4 %all-to-all-start.1 = ((f32[128,2,3,128]{3,1,2,0:T(2,128)}), f32[128,2,3,128]{3,1,2,0:T(2,128)S(1)}, u32[]{:S(2)}, u32[]{:S(2)}) async-start(f32[128,2,3,128]{3,1,2,0:T(2,128)} %scatter_fusion), calls=%async_computation.1 | async-start | bytes 786432 | tf_op jit(solution)/shard_map/all_to_all | solution.py:127
  75.0 3.8 %copy-start = (f32[64,3,128]{2,0,1:T(8,128)S(1)}, f32[64,3,128]{2,0,1:T(8,128)}, u32[]{:S(2)}) copy-start(f32[64,3,128]{2,0,1:T(8,128)} %param.13) | copy-start | bytes 294916
  305.7 33.2 %copy-start.1 = (f32[64,3,128]{2,0,1:T(8,128)}, f32[64,3,128]{2,0,1:T(8,128)S(1)}, u32[]{:S(2)}) copy-start(f32[64,3,128]{2,0,1:T(8,128)S(1)} %fusion.36) | copy-start | bytes 294916
  308.6 5.9 %collective-permute-start = (f32[8,3,128]{2,0,1:T(8,128)S(1)}, f32[8,3,128]{2,0,1:T(8,128)S(1)}, u32[]{:S(2)}, u32[]{:S(2)}) collective-permute-start(f32[8,3,128]{2,0,1:T(8,128)S(1)} %get-tuple-element.156), channel_id=1, source_target_pairs={{0,1},{1,2},{2,3},{3,4},{4,5},{5,6},{6,7},{7,8},{8,9},{9,10},{10,1... | collective-permute-start | bytes 36872 | tf_op jit(solution)/shard_map/ppermute | solution.py:31
  308.8 7.5 %collective-permute-start.1 = (f32[8,3,128]{2,0,1:T(8,128)S(1)}, f32[8,3,128]{2,0,1:T(8,128)S(1)}, u32[]{:S(2)}, u32[]{:S(2)}) collective-permute-start(f32[8,3,128]{2,0,1:T(8,128)S(1)} %get-tuple-element.155), channel_id=1, source_target_pairs={{0,2},{1,3},{2,4},{3,5},{4,6},{5,7},{6,8},{7,9},{8,10},{9,11},{10,... | collective-permute-start | bytes 36872 | tf_op jit(solution)/shard_map/ppermute | solution.py:31
  310.3 8.2 %collective-permute-start.2 = (f32[8,3,128]{2,0,1:T(8,128)S(1)}, f32[8,3,128]{2,0,1:T(8,128)S(1)}, u32[]{:S(2)}, u32[]{:S(2)}) collective-permute-start(f32[8,3,128]{2,0,1:T(8,128)S(1)} %get-tuple-element.154), channel_id=1, source_target_pairs={{0,3},{1,4},{2,5},{3,6},{4,7},{5,8},{6,9},{7,10},{8,11},{9,12},{10... | collective-permute-start | bytes 36872 | tf_op jit(solution)/shard_map/ppermute | solution.py:31
  312.2 8.3 %collective-permute-start.3 = (f32[8,3,128]{2,0,1:T(8,128)S(1)}, f32[8,3,128]{2,0,1:T(8,128)S(1)}, u32[]{:S(2)}, u32[]{:S(2)}) collective-permute-start(f32[8,3,128]{2,0,1:T(8,128)S(1)} %get-tuple-element.153), channel_id=1, source_target_pairs={{0,4},{1,5},{2,6},{3,7},{4,8},{5,9},{6,10},{7,11},{8,12},{9,13},{1... | collective-permute-start | bytes 36872 | tf_op jit(solution)/shard_map/ppermute | solution.py:31
  312.2 8.3 %collective-permute-start.4 = (f32[8,3,128]{2,0,1:T(8,128)S(1)}, f32[8,3,128]{2,0,1:T(8,128)S(1)}, u32[]{:S(2)}, u32[]{:S(2)}) collective-permute-start(f32[8,3,128]{2,0,1:T(8,128)S(1)} %get-tuple-element.152), channel_id=1, source_target_pairs={{0,5},{1,6},{2,7},{3,8},{4,9},{5,10},{6,11},{7,12},{8,13},{9,14},{... | collective-permute-start | bytes 36872 | tf_op jit(solution)/shard_map/ppermute | solution.py:31
  314.5 7.9 %collective-permute-start.5 = (f32[8,3,128]{2,0,1:T(8,128)S(1)}, f32[8,3,128]{2,0,1:T(8,128)S(1)}, u32[]{:S(2)}, u32[]{:S(2)}) collective-permute-start(f32[8,3,128]{2,0,1:T(8,128)S(1)} %get-tuple-element.151), channel_id=1, source_target_pairs={{0,6},{1,7},{2,8},{3,9},{4,10},{5,11},{6,12},{7,13},{8,14},{9,15},... | collective-permute-start | bytes 36872 | tf_op jit(solution)/shard_map/ppermute | solution.py:31
  316.3 9.8 %collective-permute-start.6 = (f32[8,3,128]{2,0,1:T(8,128)S(1)}, f32[8,3,128]{2,0,1:T(8,128)S(1)}, u32[]{:S(2)}, u32[]{:S(2)}) collective-permute-start(f32[8,3,128]{2,0,1:T(8,128)S(1)} %get-tuple-element.150), channel_id=1, source_target_pairs={{0,7},{1,8},{2,9},{3,10},{4,11},{5,12},{6,13},{7,14},{8,15},{9,0},... | collective-permute-start | bytes 36872 | tf_op jit(solution)/shard_map/ppermute | solution.py:31
  318.5 8.2 %collective-permute-start.7 = (f32[8,3,128]{2,0,1:T(8,128)S(1)}, f32[8,3,128]{2,0,1:T(8,128)S(1)}, u32[]{:S(2)}, u32[]{:S(2)}) collective-permute-start(f32[8,3,128]{2,0,1:T(8,128)S(1)} %get-tuple-element.149), channel_id=1, source_target_pairs={{0,8},{1,9},{2,10},{3,11},{4,12},{5,13},{6,14},{7,15},{8,0},{9,1},... | collective-permute-start | bytes 36872 | tf_op jit(solution)/shard_map/ppermute | solution.py:31
  320.5 6.5 %collective-permute-start.8 = (f32[8,3,128]{2,0,1:T(8,128)S(1)}, f32[8,3,128]{2,0,1:T(8,128)S(1)}, u32[]{:S(2)}, u32[]{:S(2)}) collective-permute-start(f32[8,3,128]{2,0,1:T(8,128)S(1)} %get-tuple-element.148), channel_id=1, source_target_pairs={{0,9},{1,10},{2,11},{3,12},{4,13},{5,14},{6,15},{7,0},{8,1},{9,2},... | collective-permute-start | bytes 36872 | tf_op jit(solution)/shard_map/ppermute | solution.py:31
  320.6 8.1 %collective-permute-start.9 = (f32[8,3,128]{2,0,1:T(8,128)S(1)}, f32[8,3,128]{2,0,1:T(8,128)S(1)}, u32[]{:S(2)}, u32[]{:S(2)}) collective-permute-start(f32[8,3,128]{2,0,1:T(8,128)S(1)} %get-tuple-element.147), channel_id=1, source_target_pairs={{0,10},{1,11},{2,12},{3,13},{4,14},{5,15},{6,0},{7,1},{8,2},{9,3},... | collective-permute-start | bytes 36872 | tf_op jit(solution)/shard_map/ppermute | solution.py:31
  322.4 8.9 %collective-permute-start.10 = (f32[8,3,128]{2,0,1:T(8,128)S(1)}, f32[8,3,128]{2,0,1:T(8,128)S(1)}, u32[]{:S(2)}, u32[]{:S(2)}) collective-permute-start(f32[8,3,128]{2,0,1:T(8,128)S(1)} %get-tuple-element.146), channel_id=1, source_target_pairs={{0,11},{1,12},{2,13},{3,14},{4,15},{5,0},{6,1},{7,2},{8,3},{9,4},{... | collective-permute-start | bytes 36872 | tf_op jit(solution)/shard_map/ppermute | solution.py:31
  326.1 5.2 %collective-permute-start.11 = (f32[8,3,128]{2,0,1:T(8,128)S(1)}, f32[8,3,128]{2,0,1:T(8,128)S(1)}, u32[]{:S(2)}, u32[]{:S(2)}) collective-permute-start(f32[8,3,128]{2,0,1:T(8,128)S(1)} %get-tuple-element.145), channel_id=1, source_target_pairs={{0,12},{1,13},{2,14},{3,15},{4,0},{5,1},{6,2},{7,3},{8,4},{9,5},{1... | collective-permute-start | bytes 36872 | tf_op jit(solution)/shard_map/ppermute | solution.py:31
  326.7 4.6 %collective-permute-start.12 = (f32[8,3,128]{2,0,1:T(8,128)S(1)}, f32[8,3,128]{2,0,1:T(8,128)S(1)}, u32[]{:S(2)}, u32[]{:S(2)}) collective-permute-start(f32[8,3,128]{2,0,1:T(8,128)S(1)} %get-tuple-element.144), channel_id=1, source_target_pairs={{0,13},{1,14},{2,15},{3,0},{4,1},{5,2},{6,3},{7,4},{8,5},{9,6},{10... | collective-permute-start | bytes 36872 | tf_op jit(solution)/shard_map/ppermute | solution.py:31
  327.0 4.3 %collective-permute-start.13 = (f32[8,3,128]{2,0,1:T(8,128)S(1)}, f32[8,3,128]{2,0,1:T(8,128)S(1)}, u32[]{:S(2)}, u32[]{:S(2)}) collective-permute-start(f32[8,3,128]{2,0,1:T(8,128)S(1)} %get-tuple-element.143), channel_id=1, source_target_pairs={{0,14},{1,15},{2,0},{3,1},{4,2},{5,3},{6,4},{7,5},{8,6},{9,7},{10,... | collective-permute-start | bytes 36872 | tf_op jit(solution)/shard_map/ppermute | solution.py:31
  328.6 4.1 %collective-permute-start.14 = (f32[8,3,128]{2,0,1:T(8,128)S(1)}, f32[8,3,128]{2,0,1:T(8,128)S(1)}, u32[]{:S(2)}, u32[]{:S(2)}) collective-permute-start(f32[8,3,128]{2,0,1:T(8,128)S(1)} %get-tuple-element.142), channel_id=1, source_target_pairs={{0,15},{1,0},{2,1},{3,2},{4,3},{5,4},{6,5},{7,6},{8,7},{9,8},{10,9... | collective-permute-start | bytes 36872 | tf_op jit(solution)/shard_map/ppermute | solution.py:31
Sparse Core Ops, SparseCore 0:
  10.8 54.9 all-gather.1
